TPU v7x, 32 devices: a whole 2x2x4 slice. The times are simulated.
32 devices in a mesh: rep: 4 (over x, core), shard: 8 (over z, y).
Axes of the slice: x: 2, y: 2, z: 4, core: 2. Of those that a mesh axis runs over, the one named last changes fastest.
Arguments:
- block_input: float32 [32, 256, 768], P(('rep', 'shard')), may hold values from -6 to 6
- attn_gain: bfloat16 [768], P('shard'), may hold values from 0.099609375 to 1.8984375
- attn_shift: bfloat16 [768], P('shard'), may hold values from -3 to 3
- query_weight: bfloat16 [768, 768], P('shard'), may hold values from -4 to 4
- query_bias: bfloat16 [768], P('shard'), may hold values from -3 to 3
- key_weight: bfloat16 [768, 768], P('shard'), may hold values from -4 to 4
- value_weight: bfloat16 [768, 768], P('shard'), may hold values from -0.21875 to 0.21875
- value_bias: bfloat16 [768], P('shard'), may hold values from -0.3125 to 0.3125
- out_weight: bfloat16 [768, 768], P('shard'), may hold values from -3.5 to 3.5
- out_bias: bfloat16 [768], P('shard'), may hold values from -3 to 3
- mlp_gain: bfloat16 [768], P('shard'), may hold values from 0.099609375 to 1.8984375
- mlp_shift: bfloat16 [768], P('shard'), may hold values from -3 to 3
- hidden_weight: bfloat16 [768, 3072], P('shard'), may hold values from -0.21875 to 0.21875
- hidden_bias: bfloat16 [3072], P('shard'), may hold values from -3 to 3
- proj_weight: bfloat16 [3072, 768], P('shard'), may hold values from -0.109375 to 0.109375
- proj_bias: bfloat16 [768], P('shard'), may hold values from -3 to 3
- out_cotangent: float32 [32, 256, 768], P(('rep', 'shard')), may hold values from -6 to 6
Outputs:
- block_output: float32 [32, 256, 768], P(('rep', 'shard'))
- input_grad: float32 [32, 256, 768], P(('rep', 'shard'))
- attn_gain_grad: float32 [768], P('shard')
- attn_shift_grad: float32 [768], P('shard')
- query_weight_grad: float32 [768, 768], P('shard')
- query_bias_grad: float32 [768], P('shard')
- key_weight_grad: float32 [768, 768], P('shard')
- value_weight_grad: float32 [768, 768], P('shard')
- value_bias_grad: float32 [768], P('shard')
- out_weight_grad: float32 [768, 768], P('shard')
- out_bias_grad: float32 [768], P('shard')
- mlp_gain_grad: float32 [768], P('shard')
- mlp_shift_grad: float32 [768], P('shard')
- hidden_weight_grad: float32 [768, 3072], P('shard')
- hidden_bias_grad: float32 [3072], P('shard')
- proj_weight_grad: float32 [3072, 768], P('shard')
- proj_bias_grad: float32 [768], P('shard')
All inputs are finite; a program needn't handle non-finite values.
Results may differ from a plain program's by a relative error of at most 0.02.
The roundings to bfloat16 on the way count: a program that leaves them out, or rounds other values in their place, can miss the bound.
Values may be sent and summed in bfloat16 or wider, within the bound.
A program may use at most 128 MiB of HBM per device.

v0:
```python
import jax
import jax.numpy as jnp
from jax import lax
from jax.sharding import PartitionSpec as P

HD = 64
EPS = 1e-05
ROOT_HALF = 0.7071067811865476
INV_ROOT_TWO_PI = 0.3989422804014327


def layer_norm(tokens, norm_gain, norm_shift):
    average = jnp.mean(tokens, axis=-1, keepdims=True)
    centered = tokens - average
    inv_std = lax.rsqrt(jnp.mean(centered * centered, axis=-1, keepdims=True) + EPS)
    normed = centered * inv_std
    shaped = normed * norm_gain.astype(jnp.float32) + norm_shift.astype(jnp.float32)
    return (normed, inv_std, shaped.astype(jnp.bfloat16))


def norm_grad(upstream, normed, inv_std, norm_gain):
    scaled = upstream * norm_gain.astype(jnp.float32)
    inner = (
        scaled
        - jnp.mean(scaled, axis=-1, keepdims=True)
        - normed * jnp.mean(scaled * normed, axis=-1, keepdims=True)
    )
    return (inner * inv_std, jnp.sum(upstream * normed, axis=0), jnp.sum(upstream, axis=0))


def matmul(left, right):
    return jnp.dot(left, right, preferred_element_type=jnp.float32)


def times_transposed(left, right):
    return lax.dot_general(
        left, right, (((1,), (1,)), ((), ())), preferred_element_type=jnp.float32
    )


def token_sum(left, right):
    return lax.dot_general(
        left, right, (((0,), (0,)), ((), ())), preferred_element_type=jnp.float32
    )


def gelu_parts(before):
    normal_cdf = 0.5 * (1.0 + lax.erf(before * ROOT_HALF))
    return (
        before * normal_cdf,
        normal_cdf + before * INV_ROOT_TWO_PI * jnp.exp(-0.5 * before * before),
    )


def attend(query, keys, values):
    factor = query.shape[-1] ** (-0.5)
    scores = jnp.einsum("clhd,cmhd->chlm", query, keys, preferred_element_type=jnp.float32) * factor
    row_top = jnp.max(scores, axis=-1, keepdims=True)
    log_total = row_top + jnp.log(jnp.sum(jnp.exp(scores - row_top), axis=-1, keepdims=True))
    weights = jnp.exp(scores - log_total).astype(jnp.bfloat16)
    mixed = jnp.einsum(
        "chlm,cmhd->clhd", weights, values, preferred_element_type=jnp.float32
    ).astype(jnp.bfloat16)
    return (mixed, log_total)


def attend_grad(query, keys, values, mixed, log_total, grad_mixed):
    factor = query.shape[-1] ** (-0.5)
    scores = jnp.einsum("clhd,cmhd->chlm", query, keys, preferred_element_type=jnp.float32) * factor
    weights = jnp.exp(scores - log_total)
    weights_low = weights.astype(jnp.bfloat16)
    grad_values = jnp.einsum(
        "chlm,clhd->cmhd", weights_low, grad_mixed, preferred_element_type=jnp.float32
    )
    grad_weights = jnp.einsum(
        "clhd,cmhd->chlm", grad_mixed, values, preferred_element_type=jnp.float32
    )
    delta = jnp.sum(grad_mixed.astype(jnp.float32) * mixed.astype(jnp.float32), axis=-1)
    delta = jnp.transpose(delta, (0, 2, 1))[..., None]
    grad_scores = (weights * (grad_weights - delta)).astype(jnp.bfloat16)
    grad_query = (
        jnp.einsum("chlm,cmhd->clhd", grad_scores, keys, preferred_element_type=jnp.float32)
        * factor
    )
    grad_keys = (
        jnp.einsum("chlm,clhd->cmhd", grad_scores, query, preferred_element_type=jnp.float32)
        * factor
    )
    return (grad_query, grad_keys, grad_values)


def cut_columns(matrix, likes, flat=True):
    pieces = []
    start = 0
    for like in likes:
        width = like.shape[-1]
        piece = matrix[:, start : start + width]
        pieces.append(piece.reshape(-1) if flat else piece)
        start += width
    return tuple(pieces)


def on_device(
    block_input,
    attn_gain,
    attn_shift,
    query_weight,
    query_bias,
    key_weight,
    value_weight,
    value_bias,
    out_weight,
    out_bias,
    mlp_gain,
    mlp_shift,
    hidden_weight,
    hidden_bias,
    proj_weight,
    proj_bias,
    out_cotangent,
):
    clip_count, frame_count, model_width = block_input.shape
    head_count = model_width // HD
    token_count = clip_count * frame_count

    def split_heads(matrix):
        return matrix.reshape(clip_count, frame_count, head_count, HD)

    def join_heads(tensor):
        return tensor.reshape(token_count, model_width)

    residual = block_input.reshape(token_count, model_width)
    vectors = (
        attn_gain,
        attn_shift,
        query_bias,
        value_bias,
        out_bias,
        mlp_gain,
        mlp_shift,
        proj_bias,
        hidden_bias,
    )
    squares = (query_weight, key_weight, value_weight, out_weight, hidden_weight)
    vectors_all = lax.all_gather(jnp.concatenate(vectors), "shard", axis=0, tiled=False)
    squares_all = lax.all_gather(jnp.concatenate(squares, axis=1), "shard", axis=0, tiled=True)
    proj_all = lax.all_gather(proj_weight, "shard", axis=0, tiled=True)
    (
        attn_gain_all,
        attn_shift_all,
        query_bias_all,
        value_bias_all,
        out_bias_all,
        mlp_gain_all,
        mlp_shift_all,
        proj_bias_all,
        hidden_bias_all,
    ) = cut_columns(vectors_all, vectors)
    query_all, key_all, value_all, out_all, hidden_all = cut_columns(squares_all, squares, False)
    normed_one, inv_one, input_low = layer_norm(residual, attn_gain_all, attn_shift_all)
    query_low = (matmul(input_low, query_all) + query_bias_all.astype(jnp.float32)).astype(
        jnp.bfloat16
    )
    keys_low = matmul(input_low, key_all).astype(jnp.bfloat16)
    values_low = (matmul(input_low, value_all) + value_bias_all.astype(jnp.float32)).astype(
        jnp.bfloat16
    )
    mixed, log_total = attend(
        split_heads(query_low), split_heads(keys_low), split_heads(values_low)
    )
    mixed_rows = join_heads(mixed)
    middle = residual + matmul(mixed_rows, out_all) + out_bias_all.astype(jnp.float32)
    normed_two, inv_two, middle_low = layer_norm(middle, mlp_gain_all, mlp_shift_all)
    before_act = matmul(middle_low, hidden_all) + hidden_bias_all.astype(jnp.float32)
    activated, slope = gelu_parts(before_act)
    act_low = activated.astype(jnp.bfloat16)
    block_output = middle + matmul(act_low, proj_all) + proj_bias_all.astype(jnp.float32)
    upstream = out_cotangent.reshape(token_count, model_width)
    up_low = upstream.astype(jnp.bfloat16)
    proj_term = token_sum(act_low, up_low)
    proj_bias_term = jnp.sum(upstream, axis=0)
    grad_before = times_transposed(up_low, proj_all) * slope
    before_low = grad_before.astype(jnp.bfloat16)
    hidden_term = token_sum(middle_low, before_low)
    hidden_bias_term = jnp.sum(grad_before, axis=0)
    grad_normed_two = times_transposed(before_low, hidden_all)
    grad_middle_norm, mlp_gain_term, mlp_shift_term = norm_grad(
        grad_normed_two, normed_two, inv_two, mlp_gain_all
    )
    grad_middle = upstream + grad_middle_norm
    middle_grad_low = grad_middle.astype(jnp.bfloat16)
    out_term = token_sum(mixed_rows, middle_grad_low)
    out_bias_term = jnp.sum(grad_middle, axis=0)
    grad_mixed = times_transposed(middle_grad_low, out_all).astype(jnp.bfloat16)
    grad_query, grad_keys, grad_values = attend_grad(
        split_heads(query_low),
        split_heads(keys_low),
        split_heads(values_low),
        mixed,
        log_total,
        split_heads(grad_mixed),
    )
    grad_query = join_heads(grad_query)
    grad_keys = join_heads(grad_keys)
    grad_values = join_heads(grad_values)
    query_bias_term = jnp.sum(grad_query, axis=0)
    value_bias_term = jnp.sum(grad_values, axis=0)
    query_grad_low = grad_query.astype(jnp.bfloat16)
    key_grad_low = grad_keys.astype(jnp.bfloat16)
    value_grad_low = grad_values.astype(jnp.bfloat16)
    query_term = token_sum(input_low, query_grad_low)
    key_term = token_sum(input_low, key_grad_low)
    value_term = token_sum(input_low, value_grad_low)
    grad_normed_one = (
        times_transposed(query_grad_low, query_all)
        + times_transposed(key_grad_low, key_all)
        + times_transposed(value_grad_low, value_all)
    )
    grad_input_norm, attn_gain_term, attn_shift_term = norm_grad(
        grad_normed_one, normed_one, inv_one, attn_gain_all
    )
    input_grad = grad_middle + grad_input_norm
    shards = lax.axis_size("shard")
    vector_terms = jnp.concatenate(
        [
            term.reshape(shards, -1)
            for term in (
                attn_gain_term,
                attn_shift_term,
                query_bias_term,
                value_bias_term,
                out_bias_term,
                mlp_gain_term,
                mlp_shift_term,
                proj_bias_term,
                hidden_bias_term,
            )
        ],
        axis=1,
    )
    square_terms = jnp.concatenate(
        [
            term.astype(jnp.bfloat16)
            for term in (query_term, key_term, value_term, out_term, hidden_term)
        ],
        axis=1,
    )
    vector_owned = lax.psum(vector_terms, ("rep", "shard"))
    vector_owned = lax.dynamic_index_in_dim(
        vector_owned, lax.axis_index("shard"), 0, keepdims=False
    )
    square_owned = lax.psum_scatter(square_terms, "shard", scatter_dimension=0, tiled=True)
    proj_owned = lax.psum_scatter(
        proj_term.astype(jnp.bfloat16), "shard", scatter_dimension=0, tiled=True
    )
    square_owned = lax.psum(square_owned, "rep").astype(jnp.float32)
    proj_weight_grad = lax.psum(proj_owned, "rep").astype(jnp.float32)
    (
        attn_gain_grad,
        attn_shift_grad,
        query_bias_grad,
        value_bias_grad,
        out_bias_grad,
        mlp_gain_grad,
        mlp_shift_grad,
        proj_bias_grad,
        hidden_bias_grad,
    ) = cut_columns(vector_owned[None, :], vectors)
    query_weight_grad, key_weight_grad, value_weight_grad, out_weight_grad, hidden_weight_grad = (
        cut_columns(square_owned, squares, False)
    )
    return (
        block_output.reshape(clip_count, frame_count, model_width),
        input_grad.reshape(clip_count, frame_count, model_width),
        attn_gain_grad,
        attn_shift_grad,
        query_weight_grad,
        query_bias_grad,
        key_weight_grad,
        value_weight_grad,
        value_bias_grad,
        out_weight_grad,
        out_bias_grad,
        mlp_gain_grad,
        mlp_shift_grad,
        hidden_weight_grad,
        hidden_bias_grad,
        proj_weight_grad,
        proj_bias_grad,
    )


def solution(mesh):
    placed = (
        P(("rep", "shard"), None, None),
        P("shard"),
        P("shard"),
        P("shard", None),
        P("shard"),
        P("shard", None),
        P("shard", None),
        P("shard"),
        P("shard", None),
        P("shard"),
        P("shard"),
        P("shard"),
        P("shard", None),
        P("shard"),
        P("shard", None),
        P("shard"),
        P(("rep", "shard"), None, None),
    )
    return jax.shard_map(
        on_device,
        mesh=mesh,
        in_specs=placed,
        out_specs=(
            P(("rep", "shard"), None, None),
            P(("rep", "shard"), None, None),
            P("shard"),
            P("shard"),
            P("shard", None),
            P("shard"),
            P("shard", None),
            P("shard", None),
            P("shard"),
            P("shard", None),
            P("shard"),
            P("shard"),
            P("shard"),
            P("shard", None),
            P("shard"),
            P("shard", None),
            P("shard"),
        ),
        check_vma=False,
    )
```

profile of v0, /device:TPU:0, one launch (start us, length us, event | category | flops | bytes accessed | tf_op | source)
XLA Modules:
  0.0 555.6 jit_solution(15415747082169291236)
XLA Ops:
  14.3 33.4 %all-gather.1 = bf16[8,1,1152]{2,1,0:T(2,128)(2,1)S(1)} all-gather(bf16[1,1,1152]{2,1,0:T(2,128)(2,1)S(1)} %reshape.446), channel_id=2, replica_groups=mesh['rep'=4,'shard'=8] {'shard'}, dimensions={0}, use_global_device_ids=true | all-gather | bytes 20736 | tf_op jit(solution)/shard_map/all_gather | solution.py:145
  52.7 101.0 %all-gather.5.cloned.1.call-done = bf16[768,6144]{1,0:T(8,128)(2,1)} async-done(((bf16[96,6144]{1,0:T(8,128)(2,1)}), bf16[768,6144]{1,0:T(8,128)(2,1)}) %all-gather.5.cloned.1.call-update) | async-done | bytes 9437200 | tf_op jit(solution)/shard_map/all_gather | solution.py:146
  153.7 1.7 fusion.17
  156.4 1.7 convolution_convert_fusion.8
  158.3 1.9 fusion.16
  161.1 1.8 multiply_reduce_fusion
  166.7 3.3 multiply_convert_fusion.1
  171.3 3.7 fusion.47
  175.3 2.1 fusion.31
  177.4 56.0 %all-gather.7.cloned.1.call-done = bf16[3072,768]{1,0:T(8,128)(2,1)} async-done(((bf16[384,768]{1,0:T(8,128)(2,1)}), bf16[3072,768]{1,0:T(8,128)(2,1)}) %all-gather.7.cloned.1.call-update) | async-done | bytes 4718608 | tf_op jit(solution)/shard_map/all_gather | solution.py:147
  233.4 6.1 %fusion.45 = (f32[3072]{0:T(1024)}, bf16[256,3072]{1,0:T(8,128)(2,1)S(1)}) fusion(f32[256,3072]{1,0:T(8,128)} %get-tuple-element.58, bf16[3072,768]{1,0:T(8,128)(2,1)} %all-gather.7.cloned.1.call-done, f32[1,256,768]{2,1,0:T(8,128)} %param.33), kind=kOutput, calls=%fused_computation.119 | convolution fusion | flops 1216607232 | bytes 10235904 | tf_op jit(solution)/shard_map/dot_general | solution.py:36
  239.5 5.2 multiply_reduce_fusion.1
  246.5 2.5 convolution_convert_fusion.6
  249.1 1.9 copy.70
  251.0 2.0 copy.71
  253.0 2.7 convolution_convert_fusion.5
  255.7 2.4 copy.79
  258.1 2.4 fusion.42
  262.8 2.4 copy.78
  266.5 2.1 multiply_convert_fusion
  272.3 2.1 fusion.43
  276.6 1.7 copy.76
  283.1 3.8 fusion
  296.9 1.8 fusion.23
  298.7 1.8 convolution_add_fusion.1
  300.6 2.8 multiply_reduce_fusion.2
  305.7 40.4 %psum.21 = f32[8,1152]{1,0:T(8,128)S(1)} all-reduce(f32[8,1152]{1,0:T(8,128)S(1)} %concatenate.14), channel_id=1, replica_groups=mesh['rep'=4,'shard'=8] {'rep','shard'}, use_global_device_ids=true, to_apply=%region_20.0 | all-reduce | flops 9216 | bytes 73728 | tf_op jit(solution)/shard_map/psum | solution.py:248
  347.5 149.5 %reduce-scatter.3.cloned.1.call-done = bf16[96,6144]{1,0:T(8,128)(2,1)} async-done(((bf16[768,6144]{1,0:T(8,128)(2,1)}), bf16[96,6144]{1,0:T(8,128)(2,1)}) %reduce-scatter.3.cloned.1.call-update) | async-done | bytes 1179664 | tf_op jit(solution)/shard_map/reduce_scatter | solution.py:252
  498.4 1.8 add_bitcast_fusion
  500.2 4.6 fusion.15
  504.8 39.8 %all-reduce.3.cloned.1.call-done = (bf16[96,6144]{1,0:T(8,128)(2,1)}, bf16[384,768]{1,0:T(8,128)(2,1)}) async-done(((bf16[96,6144]{1,0:T(8,128)(2,1)}, bf16[384,768]{1,0:T(8,128)(2,1)}), (bf16[96,6144]{1,0:T(8,128)(2,1)}, bf16[384,768]{1,0:T(8,128)(2,1)})) %all-reduce.3.cloned.1.call-update) | async-done | bytes 1769488 | tf_op jit(solution)/shard_map/psum | solution.py:256
  544.6 2.3 slice.130
  (202 shorter events, 52.1 us)
Async XLA Ops:
  7.2 6.9 %copy-start.61 = (bf16[96]{0:T(256)(128)(2,1)S(1)}, bf16[96]{0:T(256)(128)(2,1)}, u32[]{:S(2)}) copy-start(bf16[96]{0:T(256)(128)(2,1)} %param.32) | copy-start | bytes 580
  7.2 6.9 %copy-start.53 = (bf16[384]{0:T(512)(128)(2,1)S(1)}, bf16[384]{0:T(512)(128)(2,1)}, u32[]{:S(2)}) copy-start(bf16[384]{0:T(512)(128)(2,1)} %param.30) | copy-start | bytes 2308
  7.2 6.9 %copy-start.60 = (bf16[96]{0:T(256)(128)(2,1)S(1)}, bf16[96]{0:T(256)(128)(2,1)}, u32[]{:S(2)}) copy-start(bf16[96]{0:T(256)(128)(2,1)} %param.28) | copy-start | bytes 580
  7.2 6.9 %copy-start.59 = (bf16[96]{0:T(256)(128)(2,1)S(1)}, bf16[96]{0:T(256)(128)(2,1)}, u32[]{:S(2)}) copy-start(bf16[96]{0:T(256)(128)(2,1)} %param.27) | copy-start | bytes 580
  7.2 6.9 %copy-start.58 = (bf16[96]{0:T(256)(128)(2,1)S(1)}, bf16[96]{0:T(256)(128)(2,1)}, u32[]{:S(2)}) copy-start(bf16[96]{0:T(256)(128)(2,1)} %param.26) | copy-start | bytes 580
  7.2 6.9 %copy-start.57 = (bf16[96]{0:T(256)(128)(2,1)S(1)}, bf16[96]{0:T(256)(128)(2,1)}, u32[]{:S(2)}) copy-start(bf16[96]{0:T(256)(128)(2,1)} %param.24) | copy-start | bytes 580
  7.3 6.9 %copy-start.56 = (bf16[96]{0:T(256)(128)(2,1)S(1)}, bf16[96]{0:T(256)(128)(2,1)}, u32[]{:S(2)}) copy-start(bf16[96]{0:T(256)(128)(2,1)} %param.21) | copy-start | bytes 580
  7.3 6.9 %copy-start.55 = (bf16[96]{0:T(256)(128)(2,1)S(1)}, bf16[96]{0:T(256)(128)(2,1)}, u32[]{:S(2)}) copy-start(bf16[96]{0:T(256)(128)(2,1)} %param.19) | copy-start | bytes 580
  7.3 6.9 %copy-start.54 = (bf16[96]{0:T(256)(128)(2,1)S(1)}, bf16[96]{0:T(256)(128)(2,1)}, u32[]{:S(2)}) copy-start(bf16[96]{0:T(256)(128)(2,1)} %param.18) | copy-start | bytes 580
  7.3 44.0 %copy-start = (f32[1,256,768]{2,1,0:T(8,128)S(1)}, f32[1,256,768]{2,1,0:T(8,128)}, u32[]{:S(2)}) copy-start(f32[1,256,768]{2,1,0:T(8,128)} %param.17) | copy-start | bytes 2359300
  7.3 146.4 %all-gather.5.cloned.1.call-start = ((), (), s32[]{:S(2)}) async-start(), calls=%async_computation.2 | async-start | bytes 10616832 | tf_op jit(solution)/shard_map/all_gather | solution.py:146
  13.3 220.2 %all-gather.7.cloned.1.call-start = ((), (), s32[]{:S(2)}) async-start(), calls=%async_computation.3 | async-start | bytes 5308416 | tf_op jit(solution)/shard_map/all_gather | solution.py:147
  14.0 333.5 %reduce-scatter.5.cloned.1.call-start = ((), (), s32[]{:S(2)}) async-start(), calls=%async_computation.5 | async-start | bytes 5308416 | tf_op jit(solution)/shard_map/reduce_scatter | solution.py:253
  49.7 108.4 %copy-start.33 = (f32[768]{0:T(1024)}, f32[768]{0:T(1024)S(1)}, u32[]{:S(2)}) copy-start(f32[768]{0:T(1024)S(1)} %reshape.435) | copy-start | bytes 9220
  50.4 107.7 %copy-start.35 = (f32[768]{0:T(1024)}, f32[768]{0:T(1024)S(1)}, u32[]{:S(2)}) copy-start(f32[768]{0:T(1024)S(1)} %reshape.436) | copy-start | bytes 9220
  158.3 4.7 copy-start.25
  166.7 4.6 copy-start.7
  175.0 322.0 %reduce-scatter.3.cloned.1.call-start = ((), (), s32[]{:S(2)}) async-start(), calls=%async_computation.4 | async-start | bytes 10616832 | tf_op jit(solution)/shard_map/reduce_scatter | solution.py:252
  233.4 6.1 %copy-start.11 = (f32[256,768]{1,0:T(8,128)S(1)}, f32[256,768]{1,0:T(8,128)}, u32[]{:S(2)}) copy-start(f32[256,768]{1,0:T(8,128)} %copy-done.10) | copy-start | bytes 2359300
  233.4 6.1 %copy-start.39 = (f32[768]{0:T(1024)S(1)}, f32[768]{0:T(1024)}, u32[]{:S(2)}) copy-start(f32[768]{0:T(1024)} %reshape.440) | copy-start | bytes 9220
  233.4 6.1 %copy-start.45 = (f32[256]{0:T(256)S(1)}, f32[256]{0:T(256)}, u32[]{:S(2)}) copy-start(f32[256]{0:T(256)} %copy-done.44) | copy-start | bytes 3076
  233.4 6.1 %copy-start.48 = (f32[256]{0:T(256)S(1)}, f32[256]{0:T(256)}, u32[]{:S(2)}) copy-start(f32[256]{0:T(256)} %copy-done.47) | copy-start | bytes 3076
  239.5 5.2 copy-start.62
  239.5 5.2 copy-start.8
  286.9 10.0 %copy-start.24 = (bf16[1,256,12,64]{1,3,2,0:T(8,128)(2,1)S(1)}, bf16[1,256,12,64]{1,3,2,0:T(8,128)(2,1)}, u32[]{:S(2)}) copy-start(bf16[1,256,12,64]{1,3,2,0:T(8,128)(2,1)} %copy-done.23) | copy-start | bytes 1179652
  287.0 11.8 %copy-start.22 = (bf16[12,64,256]{2,1,0:T(8,128)(2,1)S(1)}, bf16[12,64,256]{2,1,0:T(8,128)(2,1)}, u32[]{:S(2)}) copy-start(bf16[12,64,256]{2,1,0:T(8,128)(2,1)} %copy-done.21) | copy-start | bytes 1179652
  287.0 257.6 %all-reduce.3.cloned.1.call-start = ((), (), s32[]{:S(2)}) async-start(), calls=%async_computation.6 | async-start | bytes 3538944 | tf_op jit(solution)/shard_map/psum | solution.py:256
  288.1 12.5 %copy-start.2 = (f32[1,256,768]{2,1,0:T(8,128)S(1)}, f32[1,256,768]{2,1,0:T(8,128)}, u32[]{:S(2)}) copy-start(f32[1,256,768]{2,1,0:T(8,128)} %param.17) | copy-start | bytes 2359300
  288.1 12.5 %copy-start.30 = (bf16[1,256,12,64]{1,3,2,0:T(8,128)(2,1)S(1)}, bf16[1,256,12,64]{1,3,2,0:T(8,128)(2,1)}, u32[]{:S(2)}) copy-start(bf16[1,256,12,64]{1,3,2,0:T(8,128)(2,1)} %copy-done.29) | copy-start | bytes 1179652
  288.1 12.5 %copy-start.34 = (f32[768]{0:T(1024)S(1)}, f32[768]{0:T(1024)}, u32[]{:S(2)}) copy-start(f32[768]{0:T(1024)} %copy-done.33) | copy-start | bytes 9220
  300.6 197.8 %copy-start.6 = (f32[256,768]{1,0:T(8,128)S(1)}, f32[256,768]{1,0:T(8,128)}, u32[]{:S(2)}) copy-start(f32[256,768]{1,0:T(8,128)} %copy-done.5) | copy-start | bytes 2359300
  303.4 196.8 %copy-start.52 = (f32[768]{0:T(1024)S(1)}, f32[768]{0:T(1024)}, u32[]{:S(2)}) copy-start(f32[768]{0:T(1024)} %reshape.443) | copy-start | bytes 9220
  (37 other events, 100.6 us)
Sparse Core Ops, SparseCore 0:
  13.4 140.2 all-gather.4
  155.9 77.5 all-gather.6
  237.1 94.7 reduce-scatter.4
  335.3 161.7 reduce-scatter.2
  499.4 45.1 all-reduce.2
where the time goes:
time: 557 us; the launch traced here: 556 us
  waiting for transfers between devices  347 us (62%)
  blocking collectives  73.9 us (13%)
  matrix products  57.4 us (10%)
  local copies, waits for them, and re-layouts  51.4 us (9%)
  between operations  14.5 us (3%)
  other arithmetic  10.7 us (2%)
    reduce_scatter x1, waiting for transfers between devices, on_device(): lax.psum_scatter(square_terms, 'shard', scatter_dimension=0, tiled=True)  150 us
    all_gather x1, waiting for transfers between devices, on_device(): lax.all_gather(jnp.concatenate(squares, axis=1), 'shard', axis=0, tiled=T...  101 us
    all_gather x1, waiting for transfers between devices, on_device(): proj_all = lax.all_gather(proj_weight, 'shard', axis=0, tiled=True)  56 us
    psum x1, blocking collectives, on_device(): vector_owned = lax.psum(vector_terms, ('rep', 'shard'))  40.4 us
    psum x1, waiting for transfers between devices, on_device(): square_owned = lax.psum(square_owned, 'rep').astype(jnp.float32)  39.8 us
    all_gather x1, blocking collectives, on_device(): lax.all_gather(jnp.concatenate(vectors), 'shard', axis=0, tiled=False)  33.4 us
    dot_general x6, matrix products, times_transposed(): lax.dot_general(left, right, (((1,), (1,)), ((), ())), preferred_element_...  20.2 us
    unnamed x138, local copies, waits for them, and re-layouts  17.6 us
  transfers between devices with their start and end apart: 5, of which 4 were waited for; matrix products, arithmetic and copies ran while one was open for 18% of the time, Pallas kernels for 0%

commit v1 on v0

--- a/solution.py
+++ b/solution.py
@@ -245,7 +245,8 @@
         ],
         axis=1,
     )
-    vector_owned = lax.psum(vector_terms, ("rep", "shard"))
+    half = lax.psum(vector_terms, "rep")
+    vector_owned = lax.psum(half, "shard")
     vector_owned = lax.dynamic_index_in_dim(
         vector_owned, lax.axis_index("shard"), 0, keepdims=False
     )

time: 557 us -> 557 us (level)
  waiting for transfers between devices: 347 us -> 339 us
  blocking collectives: 73.9 us -> 81.7 us
    reduce_scatter x1, waiting for transfers between devices: 150 us -> 142 us  [on_device(): lax.psum_scatter(square_terms, 'shard', scatter_dimension=0, tiled=True)]
    psum x1 -> x2, blocking collectives: 40.4 us -> 48.2 us  [the longest x1 37.4 us: on_device(): vector_owned = lax.psum(half, 'shard')]
where the time goes in v1:
time: 557 us; the launch traced here: 556 us
  waiting for transfers between devices  339 us (61%)
  blocking collectives  81.7 us (15%)
  matrix products  57.3 us (10%)
  local copies, waits for them, and re-layouts  51.6 us (9%)
  between operations  14.5 us (3%)
  other arithmetic  10.8 us (2%)
    reduce_scatter x1, waiting for transfers between devices, on_device(): lax.psum_scatter(square_terms, 'shard', scatter_dimension=0, tiled=True)  142 us
    all_gather x1, waiting for transfers between devices, on_device(): lax.all_gather(jnp.concatenate(squares, axis=1), 'shard', axis=0, tiled=T...  101 us
    all_gather x1, waiting for transfers between devices, on_device(): proj_all = lax.all_gather(proj_weight, 'shard', axis=0, tiled=True)  56 us
    psum x1, waiting for transfers between devices, on_device(): square_owned = lax.psum(square_owned, 'rep').astype(jnp.float32)  39.8 us
    psum x1, blocking collectives, on_device(): vector_owned = lax.psum(half, 'shard')  37.4 us
    all_gather x1, blocking collectives, on_device(): lax.all_gather(jnp.concatenate(vectors), 'shard', axis=0, tiled=False)  33.4 us
    dot_general x6, matrix products, times_transposed(): lax.dot_general(left, right, (((1,), (1,)), ((), ())), preferred_element_...  20.2 us
    unnamed x138, local copies, waits for them, and re-layouts  17.9 us
  transfers between devices with their start and end apart: 5, of which 4 were waited for; matrix products, arithmetic and copies ran while one was open for 18% of the time, Pallas kernels for 0%

profile of v1, /device:TPU:0, one launch (start us, length us, event | category | flops | bytes accessed | tf_op | source)
XLA Modules:
  0.0 555.5 jit_solution(8204235051085811143)
XLA Ops:
  14.3 33.4 %all-gather.1 = bf16[8,1,1152]{2,1,0:T(2,128)(2,1)S(1)} all-gather(bf16[1,1,1152]{2,1,0:T(2,128)(2,1)S(1)} %reshape.446), channel_id=2, replica_groups=mesh['rep'=4,'shard'=8] {'shard'}, dimensions={0}, use_global_device_ids=true | all-gather | bytes 20736 | tf_op jit(solution)/shard_map/all_gather | solution.py:145
  52.8 100.9 %all-gather.5.cloned.1.call-done = bf16[768,6144]{1,0:T(8,128)(2,1)} async-done(((bf16[96,6144]{1,0:T(8,128)(2,1)}), bf16[768,6144]{1,0:T(8,128)(2,1)}) %all-gather.5.cloned.1.call-update) | async-done | bytes 9437200 | tf_op jit(solution)/shard_map/all_gather | solution.py:146
  153.7 1.7 fusion.17
  156.4 1.7 convolution_convert_fusion.8
  158.3 1.9 fusion.16
  161.1 1.8 multiply_reduce_fusion
  166.7 3.4 multiply_convert_fusion.1
  171.4 3.7 fusion.47
  175.3 2.1 fusion.31
  177.4 56.0 %all-gather.7.cloned.1.call-done = bf16[3072,768]{1,0:T(8,128)(2,1)} async-done(((bf16[384,768]{1,0:T(8,128)(2,1)}), bf16[3072,768]{1,0:T(8,128)(2,1)}) %all-gather.7.cloned.1.call-update) | async-done | bytes 4718608 | tf_op jit(solution)/shard_map/all_gather | solution.py:147
  233.4 6.1 %fusion.45 = (f32[3072]{0:T(1024)}, bf16[256,3072]{1,0:T(8,128)(2,1)S(1)}) fusion(f32[256,3072]{1,0:T(8,128)} %get-tuple-element.58, bf16[3072,768]{1,0:T(8,128)(2,1)} %all-gather.7.cloned.1.call-done, f32[1,256,768]{2,1,0:T(8,128)} %param.33), kind=kOutput, calls=%fused_computation.119 | convolution fusion | flops 1216607232 | bytes 10235904 | tf_op jit(solution)/shard_map/dot_general | solution.py:36
  239.5 5.2 multiply_reduce_fusion.1
  246.6 2.5 convolution_convert_fusion.6
  249.1 1.9 copy.70
  251.0 2.0 copy.71
  253.1 2.7 convolution_convert_fusion.5
  255.7 2.4 copy.79
  258.1 2.4 fusion.42
  262.8 2.4 copy.78
  266.5 2.1 multiply_convert_fusion
  272.3 2.1 fusion.43
  283.3 3.8 fusion
  297.0 1.8 fusion.23
  298.8 1.8 convolution_add_fusion.1
  300.7 2.8 multiply_reduce_fusion.2
  305.8 10.9 %psum.28 = f32[8,1152]{1,0:T(8,128)S(1)} all-reduce(f32[8,1152]{1,0:T(8,128)S(1)} %concatenate.14), channel_id=1, replica_groups=mesh['rep'=4,'shard'=8] {'rep'}, use_global_device_ids=true, to_apply=%region_20.0 | all-reduce | flops 9216 | bytes 73728 | tf_op jit(solution)/shard_map/psum | solution.py:248
  316.7 37.4 %psum.29 = f32[8,1152]{1,0:T(8,128)S(1)} all-reduce(f32[8,1152]{1,0:T(8,128)S(1)} %psum.28), channel_id=1, replica_groups=mesh['rep'=4,'shard'=8] {'shard'}, use_global_device_ids=true, to_apply=%region_21.0 | all-reduce | flops 9216 | bytes 73728 | tf_op jit(solution)/shard_map/psum | solution.py:249
  355.4 141.6 %reduce-scatter.3.cloned.1.call-done = bf16[96,6144]{1,0:T(8,128)(2,1)} async-done(((bf16[768,6144]{1,0:T(8,128)(2,1)}), bf16[96,6144]{1,0:T(8,128)(2,1)}) %reduce-scatter.3.cloned.1.call-update) | async-done | bytes 1179664 | tf_op jit(solution)/shard_map/reduce_scatter | solution.py:253
  498.3 1.8 add_bitcast_fusion
  500.2 4.6 fusion.15
  504.8 39.8 %all-reduce.3.cloned.1.call-done = (bf16[96,6144]{1,0:T(8,128)(2,1)}, bf16[384,768]{1,0:T(8,128)(2,1)}) async-done(((bf16[96,6144]{1,0:T(8,128)(2,1)}, bf16[384,768]{1,0:T(8,128)(2,1)}), (bf16[96,6144]{1,0:T(8,128)(2,1)}, bf16[384,768]{1,0:T(8,128)(2,1)})) %all-reduce.3.cloned.1.call-update) | async-done | bytes 1769488 | tf_op jit(solution)/shard_map/psum | solution.py:257
  544.6 2.3 slice.130
  (203 shorter events, 54.0 us)
Async XLA Ops:
  7.2 6.9 %copy-start.61 = (bf16[96]{0:T(256)(128)(2,1)S(1)}, bf16[96]{0:T(256)(128)(2,1)}, u32[]{:S(2)}) copy-start(bf16[96]{0:T(256)(128)(2,1)} %param.32) | copy-start | bytes 580
  7.2 6.9 %copy-start.53 = (bf16[384]{0:T(512)(128)(2,1)S(1)}, bf16[384]{0:T(512)(128)(2,1)}, u32[]{:S(2)}) copy-start(bf16[384]{0:T(512)(128)(2,1)} %param.30) | copy-start | bytes 2308
  7.2 6.9 %copy-start.60 = (bf16[96]{0:T(256)(128)(2,1)S(1)}, bf16[96]{0:T(256)(128)(2,1)}, u32[]{:S(2)}) copy-start(bf16[96]{0:T(256)(128)(2,1)} %param.28) | copy-start | bytes 580
  7.2 6.9 %copy-start.59 = (bf16[96]{0:T(256)(128)(2,1)S(1)}, bf16[96]{0:T(256)(128)(2,1)}, u32[]{:S(2)}) copy-start(bf16[96]{0:T(256)(128)(2,1)} %param.27) | copy-start | bytes 580
  7.2 6.9 %copy-start.58 = (bf16[96]{0:T(256)(128)(2,1)S(1)}, bf16[96]{0:T(256)(128)(2,1)}, u32[]{:S(2)}) copy-start(bf16[96]{0:T(256)(128)(2,1)} %param.26) | copy-start | bytes 580
  7.2 6.9 %copy-start.57 = (bf16[96]{0:T(256)(128)(2,1)S(1)}, bf16[96]{0:T(256)(128)(2,1)}, u32[]{:S(2)}) copy-start(bf16[96]{0:T(256)(128)(2,1)} %param.24) | copy-start | bytes 580
  7.3 6.9 %copy-start.56 = (bf16[96]{0:T(256)(128)(2,1)S(1)}, bf16[96]{0:T(256)(128)(2,1)}, u32[]{:S(2)}) copy-start(bf16[96]{0:T(256)(128)(2,1)} %param.21) | copy-start | bytes 580
  7.3 6.9 %copy-start.55 = (bf16[96]{0:T(256)(128)(2,1)S(1)}, bf16[96]{0:T(256)(128)(2,1)}, u32[]{:S(2)}) copy-start(bf16[96]{0:T(256)(128)(2,1)} %param.19) | copy-start | bytes 580
  7.3 6.9 %copy-start.54 = (bf16[96]{0:T(256)(128)(2,1)S(1)}, bf16[96]{0:T(256)(128)(2,1)}, u32[]{:S(2)}) copy-start(bf16[96]{0:T(256)(128)(2,1)} %param.18) | copy-start | bytes 580
  7.3 44.0 %copy-start = (f32[1,256,768]{2,1,0:T(8,128)S(1)}, f32[1,256,768]{2,1,0:T(8,128)}, u32[]{:S(2)}) copy-start(f32[1,256,768]{2,1,0:T(8,128)} %param.17) | copy-start | bytes 2359300
  7.3 146.4 %all-gather.5.cloned.1.call-start = ((), (), s32[]{:S(2)}) async-start(), calls=%async_computation.2 | async-start | bytes 10616832 | tf_op jit(solution)/shard_map/all_gather | solution.py:146
  13.3 220.2 %all-gather.7.cloned.1.call-start = ((), (), s32[]{:S(2)}) async-start(), calls=%async_computation.3 | async-start | bytes 5308416 | tf_op jit(solution)/shard_map/all_gather | solution.py:147
  14.0 341.4 %reduce-scatter.5.cloned.1.call-start = ((), (), s32[]{:S(2)}) async-start(), calls=%async_computation.5 | async-start | bytes 5308416 | tf_op jit(solution)/shard_map/reduce_scatter | solution.py:254
  49.7 108.4 %copy-start.33 = (f32[768]{0:T(1024)}, f32[768]{0:T(1024)S(1)}, u32[]{:S(2)}) copy-start(f32[768]{0:T(1024)S(1)} %reshape.435) | copy-start | bytes 9220
  50.4 107.7 %copy-start.35 = (f32[768]{0:T(1024)}, f32[768]{0:T(1024)S(1)}, u32[]{:S(2)}) copy-start(f32[768]{0:T(1024)S(1)} %reshape.436) | copy-start | bytes 9220
  158.3 4.7 copy-start.25
  166.7 4.6 copy-start.7
  175.1 321.9 %reduce-scatter.3.cloned.1.call-start = ((), (), s32[]{:S(2)}) async-start(), calls=%async_computation.4 | async-start | bytes 10616832 | tf_op jit(solution)/shard_map/reduce_scatter | solution.py:253
  233.4 6.1 %copy-start.11 = (f32[256,768]{1,0:T(8,128)S(1)}, f32[256,768]{1,0:T(8,128)}, u32[]{:S(2)}) copy-start(f32[256,768]{1,0:T(8,128)} %copy-done.10) | copy-start | bytes 2359300
  233.4 6.1 %copy-start.39 = (f32[768]{0:T(1024)S(1)}, f32[768]{0:T(1024)}, u32[]{:S(2)}) copy-start(f32[768]{0:T(1024)} %reshape.440) | copy-start | bytes 9220
  233.4 6.1 %copy-start.45 = (f32[256]{0:T(256)S(1)}, f32[256]{0:T(256)}, u32[]{:S(2)}) copy-start(f32[256]{0:T(256)} %copy-done.44) | copy-start | bytes 3076
  233.4 6.1 %copy-start.48 = (f32[256]{0:T(256)S(1)}, f32[256]{0:T(256)}, u32[]{:S(2)}) copy-start(f32[256]{0:T(256)} %copy-done.47) | copy-start | bytes 3076
  239.5 5.2 copy-start.62
  239.5 5.2 copy-start.8
  287.1 10.0 %copy-start.24 = (bf16[1,256,12,64]{1,3,2,0:T(8,128)(2,1)S(1)}, bf16[1,256,12,64]{1,3,2,0:T(8,128)(2,1)}, u32[]{:S(2)}) copy-start(bf16[1,256,12,64]{1,3,2,0:T(8,128)(2,1)} %copy-done.23) | copy-start | bytes 1179652
  287.1 11.7 %copy-start.22 = (bf16[12,64,256]{2,1,0:T(8,128)(2,1)S(1)}, bf16[12,64,256]{2,1,0:T(8,128)(2,1)}, u32[]{:S(2)}) copy-start(bf16[12,64,256]{2,1,0:T(8,128)(2,1)} %copy-done.21) | copy-start | bytes 1179652
  287.1 257.5 %all-reduce.3.cloned.1.call-start = ((), (), s32[]{:S(2)}) async-start(), calls=%async_computation.6 | async-start | bytes 3538944 | tf_op jit(solution)/shard_map/psum | solution.py:257
  288.2 12.5 %copy-start.2 = (f32[1,256,768]{2,1,0:T(8,128)S(1)}, f32[1,256,768]{2,1,0:T(8,128)}, u32[]{:S(2)}) copy-start(f32[1,256,768]{2,1,0:T(8,128)} %param.17) | copy-start | bytes 2359300
  288.2 12.5 %copy-start.30 = (bf16[1,256,12,64]{1,3,2,0:T(8,128)(2,1)S(1)}, bf16[1,256,12,64]{1,3,2,0:T(8,128)(2,1)}, u32[]{:S(2)}) copy-start(bf16[1,256,12,64]{1,3,2,0:T(8,128)(2,1)} %copy-done.29) | copy-start | bytes 1179652
  288.2 12.5 %copy-start.34 = (f32[768]{0:T(1024)S(1)}, f32[768]{0:T(1024)}, u32[]{:S(2)}) copy-start(f32[768]{0:T(1024)} %copy-done.33) | copy-start | bytes 9220
  300.7 197.7 %copy-start.6 = (f32[256,768]{1,0:T(8,128)S(1)}, f32[256,768]{1,0:T(8,128)}, u32[]{:S(2)}) copy-start(f32[256,768]{1,0:T(8,128)} %copy-done.5) | copy-start | bytes 2359300
  303.4 196.7 %copy-start.52 = (f32[768]{0:T(1024)S(1)}, f32[768]{0:T(1024)}, u32[]{:S(2)}) copy-start(f32[768]{0:T(1024)} %reshape.443) | copy-start | bytes 9220
  (37 other events, 101.7 us)
Sparse Core Ops, SparseCore 0:
  13.4 140.2 all-gather.4
  155.9 77.5 all-gather.6
  237.1 94.6 reduce-scatter.4
  335.2 161.7 reduce-scatter.2
  499.4 45.1 all-reduce.2
